TPU v7x, 256 devices: a whole 4x4x8 slice. The times are simulated.
256 devices in a mesh: tm: 32 (over x, y, core), space: 8 (over z).
Axes of the slice: x: 4, y: 4, z: 8, core: 2. Of those that a mesh axis runs over, the one named last changes fastest.
Arguments:
- snapshots: bfloat16 [512, 524288], P('tm', 'space'), may hold values from -6 to 6
- block_lists: int32 [8192, 2], P(('tm', 'space')), may hold values from 0 to 8191
- tile_counts: int32 [8192], P(('tm', 'space')), may hold values from 1 to 2
- remap_weights: bfloat16 [8192, 64, 128], P(('tm', 'space')), may hold values from -0.5 to 0.5
- basis: bfloat16 [524288, 1024], P(('tm', 'space')), may hold values from -6 to 6
- variances: float32 [1024], replicated, may hold values from 0.3 to 3
Outputs:
- coeffs: float32 [1024, 512], P('space')
- rotated: bfloat16 [524288, 1024], P(('tm', 'space'))
Inputs may be any that keep to these rules, and one draw needn't show every extreme that they name: `block_lists`: slots at or beyond a tile's count carry no weight.
All inputs are finite; a program needn't handle non-finite values.
Results may differ from a plain program's by a relative error of at most 0.0043.
Values may be sent and summed in bfloat16 or wider, within the bound.
No kernel may reach another device: no remote copies, remote signals or barrier semaphores. Data moves between devices by JAX's collectives and lax.ppermute only.
A program may use at most 192 MiB of HBM per device.

v0:
```python
import math
import jax
import jax.numpy as jnp
from jax import lax
from jax.sharding import PartitionSpec as P

TILE = 64
MAXB = 2


def per_device(snapshots, block_lists, tile_counts, remap_weights, basis, variances):
    local_tiles = block_lists.shape[0]
    time_rows = snapshots.shape[0]
    tm_size = lax.axis_size("tm")
    list_column, count_column = (
        lax.all_gather(block_lists, "tm", axis=0, tiled=True),
        lax.all_gather(tile_counts, "tm", axis=0, tiled=True),
    )
    gathered = lax.all_gather(snapshots, "space", axis=1, tiled=True)
    cell_total = gathered.shape[1]
    blocks = gathered.reshape(time_rows, cell_total // TILE, TILE)
    picked = blocks[:, list_column.reshape(-1), :].reshape(
        time_rows, tm_size * local_tiles, MAXB * TILE
    )
    slot_index = jnp.arange(MAXB * TILE, dtype=jnp.int32) // TILE
    weight_column = lax.all_gather(remap_weights, "tm", axis=0, tiled=True)
    keep = slot_index[None, :] < count_column[:, None]
    masked = jnp.where(keep[:, None, :], weight_column, jnp.zeros_like(weight_column))
    remap_part = jnp.einsum("kip,tkp->kit", masked, picked, preferred_element_type=jnp.float32)
    remap_part = remap_part.astype(jnp.bfloat16).reshape(tm_size, local_tiles * TILE, time_rows)
    arrived = lax.all_to_all(remap_part, "tm", split_axis=0, concat_axis=2, tiled=True)
    remapped = arrived.reshape(local_tiles * TILE, tm_size * time_rows)
    snap_total = remapped.shape[1]
    partial_coeffs = lax.dot_general(
        basis, remapped, (((0,), (0,)), ((), ())), preferred_element_type=jnp.float32
    )
    coeffs = lax.psum(partial_coeffs, ("tm", "space")) / math.sqrt(cell_total)
    coeff_half = coeffs.astype(jnp.bfloat16)
    coeff_rows = coeffs.shape[0] // lax.axis_size("space")
    own_coeffs = lax.dynamic_slice_in_dim(
        coeffs, lax.axis_index("space") * coeff_rows, coeff_rows, 0
    )
    update = lax.dot_general(
        remapped, coeff_half, (((1,), (1,)), ((), ())), preferred_element_type=jnp.float32
    ) / math.sqrt(snap_total)
    rotated = (basis.astype(jnp.float32) * variances[None, :] + update).astype(jnp.bfloat16)
    return (own_coeffs, rotated)


def solution(mesh):
    return jax.shard_map(
        per_device,
        mesh=mesh,
        in_specs=(
            P("tm", "space"),
            P(("tm", "space"), None),
            P(("tm", "space")),
            P(("tm", "space"), None, None),
            P(("tm", "space"), None),
            P(),
        ),
        out_specs=(P("space", None), P(("tm", "space"), None)),
        check_vma=False,
    )
```

profile of v0, /device:TPU:2, one launch (start us, length us, event | category | flops | bytes accessed | tf_op | source)
XLA Modules:
  0.0 671.5 jit_solution(16009837492111305055)
XLA Ops:
  7.2 0.0 all-gather.6.cloned.1.call-start
  7.2 0.7 all-gather.6.cloned.1.call-update
  7.9 0.0 all-gather.4.cloned.1.call-start
  7.9 0.7 all-gather.4.cloned.1.call-update
  8.6 0.0 all-reduce.3.cloned.1.call-start
  8.7 24.3 %all-gather = s32[32,32,2]{1,2,0:T(2,128)S(1)} all-gather(s32[1,32,2]{1,2,0:T(2,128)} %bitcast.20), channel_id=1, replica_groups=mesh['tm'=32,'space'=8] {'tm'}, dimensions={0}, use_global_device_ids=true | all-gather | bytes 8448 | tf_op jit(solution)/shard_map/all_gather | solution.py:16
  33.0 0.3 copy.16
  33.2 0.3 reshape.86
  33.6 1.3 dynamic-slice
  35.5 0.9 dynamic-update-slice
  36.3 13.8 %all-reduce = s32[1024]{0:T(1024)S(1)} all-reduce(s32[1024]{0:T(1024)S(1)} %dynamic-update-slice), channel_id=1, replica_groups=mesh['tm'=32,'space'=8] {'tm'}, use_global_device_ids=true, to_apply=%add | all-reduce | flops 1024 | bytes 8192
  50.1 0.2 broadcast_compare_fusion
  50.4 135.1 %all-gather.6.cloned.1.call-done = bf16[16,524288]{1,0:T(8,128)(2,1)} async-done(((bf16[16,65536]{1,0:T(8,128)(2,1)}), bf16[16,524288]{1,0:T(8,128)(2,1)}) %all-gather.6.cloned.1.call-update) | async-done | bytes 16777232 | tf_op jit(solution)/shard_map/all_gather | solution.py:19
  185.5 60.5 %reshape.85 = bf16[16,8192,64]{2,1,0:T(8,128)(2,1)} reshape(bf16[16,524288]{1,0:T(8,128)(2,1)} %all-gather.6.cloned.1.call-done) | data formatting | bytes 33554432 | tf_op jit(solution)/shard_map/reshape | solution.py:21
  246.0 29.6 %copy.17 = bf16[16,8192,64]{2,0,1:T(8,128)(2,1)} copy(bf16[16,8192,64]{2,1,0:T(8,128)(2,1)} %reshape.85) | data formatting | bytes 33554432 | tf_op jit(solution)/shard_map/reshape | solution.py:21
  275.6 33.4 %gather_fusion = bf16[2048,16,64]{2,1,0:T(8,128)(2,1)} fusion(bf16[16,8192,64]{2,0,1:T(8,128)(2,1)} %copy.17, s32[2048]{0:T(1024)S(1)} %broadcast_clamp_fusion), kind=kCustom, calls=%fused_computation | custom fusion | bytes 8396800 | tf_op jit(solution)/shard_map/gather | solution.py:22
  309.0 8.8 %copy.18 = bf16[16,2048,64]{2,1,0:T(8,128)(2,1)} copy(bf16[16,2048,64]{2,0,1:T(8,128)(2,1)} %bitcast.16) | data formatting | bytes 8388608 | tf_op jit(solution)/shard_map/gather | solution.py:22
  317.8 11.3 %reshape.87 = bf16[16,1024,128]{2,1,0:T(8,128)(2,1)} reshape(bf16[16,2048,64]{2,1,0:T(8,128)(2,1)} %copy.18) | data formatting | bytes 8388608 | tf_op jit(solution)/shard_map/reshape | solution.py:22
  329.1 0.0 all-gather.4.cloned.1.call-done
  329.1 14.3 %fusion.5 = bf16[1024,64,16]{1,2,0:T(8,128)(2,1)} fusion(bf16[16,1024,128]{2,1,0:T(8,128)(2,1)} %reshape.87, bf16[1024,64,128]{2,1,0:T(8,128)(2,1)} %all-gather.4.cloned.1.call-done, pred[1024,128]{1,0:T(8,128)(4,1)S(1)} %broadcast_compare_fusion), kind=kOutput, calls=%fused_computation.7 | convolution fusion | flops 277872640 | bytes 23199744 | tf_op jit(solution)/shard_map/kip,tkp->kit/dot_general | solution.py:29
  343.3 5.3 copy.20
  348.6 5.8 reshape.88
  354.4 0.0 copy-start
  354.4 1.2 copy.21
  355.5 32.6 %all_to_all.15 = bf16[32,2048,16]{1,2,0:T(8,128)(2,1)S(1)} all-to-all(bf16[32,2048,16]{1,2,0:T(8,128)(2,1)S(1)} %copy.21), channel_id=1, replica_groups=mesh['tm'=32,'space'=8] {'tm'}, dimensions={0} | all-to-all | bytes 4194304 | tf_op jit(solution)/shard_map/all_to_all | solution.py:31
  388.2 0.0 copy-done
  388.2 3.7 convolution_bitcast_fusion
  391.9 0.0 copy-start.1
  391.9 0.0 all-reduce.3.cloned.1.call-update
  391.9 262.6 %all-reduce.3.cloned.1.call-done = f32[1024,512]{0,1:T(8,128)} async-done(((f32[1024,512]{0,1:T(8,128)}), f32[1024,512]{0,1:T(8,128)}) %all-reduce.3.cloned.1.call-update) | async-done | bytes 2097168 | tf_op jit(solution)/shard_map/psum | solution.py:37
  654.6 1.8 broadcast_multiply_fusion
  656.4 0.8 copy.22
  657.3 0.0 copy-done.1
  657.3 7.7 %add_convert_fusion = bf16[2048,1024]{1,0:T(8,128)(2,1)} fusion(bf16[2048,1024]{1,0:T(8,128)(2,1)} %param.10, bf16[2048,512]{0,1:T(8,128)(2,1)S(1)} %bitcast.18, f32[1024]{0:T(1024)S(1)} %copy-done.1, f32[1024,512]{0,1:T(8,128)} %all-reduce.3.cloned.1.call-done), kind=kOutput, calls=%fused_computation.4 | convolution fusion | flops 2159017984 | bytes 12587008 | tf_op jit(solution)/shard_map/dot_general | solution.py:43
  (5 shorter events, 0.1 us)
Async XLA Ops:
  7.2 178.3 %all-gather.6.cloned.1.call-start = ((), (), s32[]{:S(2)}) async-start(), calls=%async_computation.2 | async-start | bytes 18874368 | tf_op jit(solution)/shard_map/all_gather | solution.py:19
  7.9 321.2 %all-gather.4.cloned.1.call-start = ((), (), s32[]{:S(2)}) async-start(), calls=%async_computation.1 | async-start | bytes 17301504 | tf_op jit(solution)/shard_map/all_gather | solution.py:26
  8.6 645.9 %all-reduce.3.cloned.1.call-start = ((), (), s32[]{:S(2)}) async-start(), calls=%async_computation.3 | async-start | bytes 4194304 | tf_op jit(solution)/shard_map/psum | solution.py:37
  354.4 33.8 %copy-start = (bf16[2048,1024]{1,0:T(8,128)(2,1)S(1)}, bf16[2048,1024]{1,0:T(8,128)(2,1)}, u32[]{:S(2)}) copy-start(bf16[2048,1024]{1,0:T(8,128)(2,1)} %param.10) | copy-start | bytes 12582916
  391.9 265.4 %copy-start.1 = (f32[1024]{0:T(1024)S(1)}, f32[1024]{0:T(1024)}, u32[]{:S(2)}) copy-start(f32[1024]{0:T(1024)} %param.11) | copy-start | bytes 12292
Sparse Core Ops, SparseCore 0:
  9.8 175.6 all-gather.5
  188.0 76.1 all-gather.3
  392.0 262.4 all-reduce.2
where the time goes:
time: 673 us; the launch traced here: 671 us
  waiting for transfers between devices  399 us (59%)
  local copies, waits for them, and re-layouts  159 us (24%)
  blocking collectives  70.7 us (11%)
  matrix products  25.6 us (4%)
  between operations  14.5 us (2%)
    psum x1, waiting for transfers between devices, per_device(): coeffs = lax.psum(partial_coeffs, ('tm', 'space')) / math.sqrt(cell_total)  263 us
    all_gather x1, waiting for transfers between devices, per_device(): gathered = lax.all_gather(snapshots, 'space', axis=1, tiled=True)  135 us
    reshape x2, local copies, waits for them, and re-layouts, per_device(): blocks = gathered.reshape(time_rows, cell_total // TILE, TILE)  90.1 us
    gather x2, local copies, waits for them, and re-layouts, per_device(): blocks[:, list_column.reshape(-1), :]  42.2 us
    all_to_all x1, blocking collectives, per_device(): lax.all_to_all(remap_part, 'tm', split_axis=0, concat_axis=2, tiled=True)  32.6 us
    all_gather x1, blocking collectives, per_device(): lax.all_gather(block_lists, 'tm', axis=0, tiled=True)  24.3 us
    dot_general x1, matrix products, per_device(): jnp.einsum('kip,tkp->kit', masked, picked, preferred_element_type=jnp.flo...  14.3 us
    unnamed x1, blocking collectives  13.8 us
  transfers between devices with their start and end apart: 3, of which 2 were waited for; matrix products, arithmetic and copies ran while one was open for 22% of the time, Pallas kernels for 0%

commit v1 on v0

--- a/solution.py
+++ b/solution.py
@@ -6,6 +6,11 @@
 
 TILE = 64
 MAXB = 2
+
+
+def axis_by_axis(array, first, second):
+    half = lax.psum(array, first)
+    return lax.psum(half, second)
 
 
 def per_device(snapshots, block_lists, tile_counts, remap_weights, basis, variances):
@@ -34,7 +39,7 @@
     partial_coeffs = lax.dot_general(
         basis, remapped, (((0,), (0,)), ((), ())), preferred_element_type=jnp.float32
     )
-    coeffs = lax.psum(partial_coeffs, ("tm", "space")) / math.sqrt(cell_total)
+    coeffs = axis_by_axis(partial_coeffs, "space", "tm") / math.sqrt(cell_total)
     coeff_half = coeffs.astype(jnp.bfloat16)
     coeff_rows = coeffs.shape[0] // lax.axis_size("space")
     own_coeffs = lax.dynamic_slice_in_dim(

time: 673 us -> 612 us (0.909)
  waiting for transfers between devices: 399 us -> 336 us
    psum x1 -> x2, waiting for transfers between devices: 263 us -> 200 us  [the longest x1 119 us: axis_by_axis(): return lax.psum(half, second)]
  transfers between devices with their start and end apart: 3 -> 4, of which waited for: 2 -> 3; matrix products, arithmetic and copies ran while one was open for 22% -> 24% of each run, Pallas kernels for 0% -> 0%
where the time goes in v1:
time: 612 us; the launch traced here: 609 us
  waiting for transfers between devices  336 us (55%)
  local copies, waits for them, and re-layouts  159 us (26%)
  blocking collectives  70.7 us (12%)
  matrix products  25.6 us (4%)
  between operations  14.5 us (2%)
    all_gather x1, waiting for transfers between devices, per_device(): gathered = lax.all_gather(snapshots, 'space', axis=1, tiled=True)  135 us
    psum x1, waiting for transfers between devices, axis_by_axis(): return lax.psum(half, second)  119 us
    reshape x2, local copies, waits for them, and re-layouts, per_device(): blocks = gathered.reshape(time_rows, cell_total // TILE, TILE)  90.1 us
    psum x1, waiting for transfers between devices, axis_by_axis(): half = lax.psum(array, first)  80.7 us
    gather x2, local copies, waits for them, and re-layouts, per_device(): blocks[:, list_column.reshape(-1), :]  42.2 us
    all_to_all x1, blocking collectives, per_device(): lax.all_to_all(remap_part, 'tm', split_axis=0, concat_axis=2, tiled=True)  32.6 us
    all_gather x1, blocking collectives, per_device(): lax.all_gather(block_lists, 'tm', axis=0, tiled=True)  24.3 us
    dot_general x1, matrix products, per_device(): jnp.einsum('kip,tkp->kit', masked, picked, preferred_element_type=jnp.flo...  14.3 us
  transfers between devices with their start and end apart: 4, of which 3 were waited for; matrix products, arithmetic and copies ran while one was open for 24% of the time, Pallas kernels for 0%

profile of v1, /device:TPU:2, one launch (start us, length us, event | category | flops | bytes accessed | tf_op | source)
XLA Modules:
  0.0 609.0 jit_solution(17740730186345002430)
XLA Ops:
  7.2 0.0 all-gather.6.cloned.1.call-start
  7.2 0.7 all-gather.6.cloned.1.call-update
  7.9 0.0 all-gather.4.cloned.1.call-start
  7.9 0.7 all-gather.4.cloned.1.call-update
  8.6 0.0 all-reduce.4.cloned.1.call-start
  8.7 24.3 %all-gather = s32[32,32,2]{1,2,0:T(2,128)S(1)} all-gather(s32[1,32,2]{1,2,0:T(2,128)} %bitcast.20), channel_id=1, replica_groups=mesh['tm'=32,'space'=8] {'tm'}, dimensions={0}, use_global_device_ids=true | all-gather | bytes 8448 | tf_op jit(solution)/shard_map/all_gather | solution.py:21
  33.0 0.3 copy.16
  33.2 0.3 reshape.86
  33.6 1.3 dynamic-slice
  35.5 0.9 dynamic-update-slice
  36.3 13.8 %all-reduce = s32[1024]{0:T(1024)S(1)} all-reduce(s32[1024]{0:T(1024)S(1)} %dynamic-update-slice), channel_id=1, replica_groups=mesh['tm'=32,'space'=8] {'tm'}, use_global_device_ids=true, to_apply=%add | all-reduce | flops 1024 | bytes 8192
  50.1 0.2 broadcast_compare_fusion
  50.4 135.1 %all-gather.6.cloned.1.call-done = bf16[16,524288]{1,0:T(8,128)(2,1)} async-done(((bf16[16,65536]{1,0:T(8,128)(2,1)}), bf16[16,524288]{1,0:T(8,128)(2,1)}) %all-gather.6.cloned.1.call-update) | async-done | bytes 16777232 | tf_op jit(solution)/shard_map/all_gather | solution.py:24
  185.5 60.5 %reshape.85 = bf16[16,8192,64]{2,1,0:T(8,128)(2,1)} reshape(bf16[16,524288]{1,0:T(8,128)(2,1)} %all-gather.6.cloned.1.call-done) | data formatting | bytes 33554432 | tf_op jit(solution)/shard_map/reshape | solution.py:26
  246.0 29.6 %copy.17 = bf16[16,8192,64]{2,0,1:T(8,128)(2,1)} copy(bf16[16,8192,64]{2,1,0:T(8,128)(2,1)} %reshape.85) | data formatting | bytes 33554432 | tf_op jit(solution)/shard_map/reshape | solution.py:26
  275.6 33.4 %gather_fusion = bf16[2048,16,64]{2,1,0:T(8,128)(2,1)} fusion(bf16[16,8192,64]{2,0,1:T(8,128)(2,1)} %copy.17, s32[2048]{0:T(1024)S(1)} %broadcast_clamp_fusion), kind=kCustom, calls=%fused_computation | custom fusion | bytes 8396800 | tf_op jit(solution)/shard_map/gather | solution.py:27
  309.0 8.8 %copy.18 = bf16[16,2048,64]{2,1,0:T(8,128)(2,1)} copy(bf16[16,2048,64]{2,0,1:T(8,128)(2,1)} %bitcast.16) | data formatting | bytes 8388608 | tf_op jit(solution)/shard_map/gather | solution.py:27
  317.8 11.3 %reshape.87 = bf16[16,1024,128]{2,1,0:T(8,128)(2,1)} reshape(bf16[16,2048,64]{2,1,0:T(8,128)(2,1)} %copy.18) | data formatting | bytes 8388608 | tf_op jit(solution)/shard_map/reshape | solution.py:27
  329.1 0.0 all-gather.4.cloned.1.call-done
  329.1 14.3 %fusion.5 = bf16[1024,64,16]{1,2,0:T(8,128)(2,1)} fusion(bf16[16,1024,128]{2,1,0:T(8,128)(2,1)} %reshape.87, bf16[1024,64,128]{2,1,0:T(8,128)(2,1)} %all-gather.4.cloned.1.call-done, pred[1024,128]{1,0:T(8,128)(4,1)S(1)} %broadcast_compare_fusion), kind=kOutput, calls=%fused_computation.7 | convolution fusion | flops 277872640 | bytes 23199744 | tf_op jit(solution)/shard_map/kip,tkp->kit/dot_general | solution.py:34
  343.3 5.3 copy.20
  348.6 5.8 reshape.88
  354.4 0.0 copy-start
  354.4 1.2 copy.21
  355.5 32.6 %all_to_all.15 = bf16[32,2048,16]{1,2,0:T(8,128)(2,1)S(1)} all-to-all(bf16[32,2048,16]{1,2,0:T(8,128)(2,1)S(1)} %copy.21), channel_id=1, replica_groups=mesh['tm'=32,'space'=8] {'tm'}, dimensions={0} | all-to-all | bytes 4194304 | tf_op jit(solution)/shard_map/all_to_all | solution.py:36
  388.2 0.0 copy-done
  388.2 3.7 convolution_bitcast_fusion
  391.9 0.0 all-reduce.4.cloned.1.call-update
  391.9 0.0 copy-start.1
  391.9 0.3 all-reduce.6.cloned.1.call-start
  392.2 80.7 %all-reduce.4.cloned.1.call-done = f32[1024,512]{0,1:T(8,128)} async-done(((f32[1024,512]{0,1:T(8,128)}), f32[1024,512]{0,1:T(8,128)}) %all-reduce.4.cloned.1.call-update) | async-done | bytes 2097168 | tf_op jit(solution)/shard_map/psum | solution.py:12
  472.9 0.0 all-reduce.6.cloned.1.call-update
  472.9 119.1 %all-reduce.6.cloned.1.call-done = f32[1024,512]{0,1:T(8,128)} async-done(((f32[1024,512]{0,1:T(8,128)}), f32[1024,512]{0,1:T(8,128)}) %all-reduce.6.cloned.1.call-update) | async-done | bytes 2097168 | tf_op jit(solution)/shard_map/psum | solution.py:13
  592.0 1.8 broadcast_multiply_fusion
  593.9 0.8 copy.22
  594.7 0.0 copy-done.1
  594.7 7.7 %add_convert_fusion = bf16[2048,1024]{1,0:T(8,128)(2,1)} fusion(bf16[2048,1024]{1,0:T(8,128)(2,1)} %param.10, bf16[2048,512]{0,1:T(8,128)(2,1)S(1)} %bitcast.18, f32[1024]{0:T(1024)S(1)} %copy-done.1, f32[1024,512]{0,1:T(8,128)} %all-reduce.6.cloned.1.call-done), kind=kOutput, calls=%fused_computation.4 | convolution fusion | flops 2159017984 | bytes 12587008 | tf_op jit(solution)/shard_map/dot_general | solution.py:48
  (5 shorter events, 0.1 us)
Async XLA Ops:
  7.2 178.3 %all-gather.6.cloned.1.call-start = ((), (), s32[]{:S(2)}) async-start(), calls=%async_computation.2 | async-start | bytes 18874368 | tf_op jit(solution)/shard_map/all_gather | solution.py:24
  7.9 321.2 %all-gather.4.cloned.1.call-start = ((), (), s32[]{:S(2)}) async-start(), calls=%async_computation.1 | async-start | bytes 17301504 | tf_op jit(solution)/shard_map/all_gather | solution.py:31
  8.6 464.3 %all-reduce.4.cloned.1.call-start = ((), (), s32[]{:S(2)}) async-start(), calls=%async_computation.3 | async-start | bytes 4194304 | tf_op jit(solution)/shard_map/psum | solution.py:12
  354.4 33.8 %copy-start = (bf16[2048,1024]{1,0:T(8,128)(2,1)S(1)}, bf16[2048,1024]{1,0:T(8,128)(2,1)}, u32[]{:S(2)}) copy-start(bf16[2048,1024]{1,0:T(8,128)(2,1)} %param.10) | copy-start | bytes 12582916
  391.9 202.8 %copy-start.1 = (f32[1024]{0:T(1024)S(1)}, f32[1024]{0:T(1024)}, u32[]{:S(2)}) copy-start(f32[1024]{0:T(1024)} %param.11) | copy-start | bytes 12292
  391.9 200.1 %all-reduce.6.cloned.1.call-start = ((), (), s32[]{:S(2)}) async-start(), calls=%async_computation.4 | async-start | bytes 4194304 | tf_op jit(solution)/shard_map/psum | solution.py:13
Sparse Core Ops, SparseCore 0:
  9.8 175.6 all-gather.5
  188.0 76.1 all-gather.3
  392.0 80.8 all-reduce.3
  476.0 115.9 all-reduce.5
